TPU v7x, 512 devices: a whole 4x8x8 slice. The times are simulated.
512 devices in a mesh: pix: 32 (over x, y), tm: 16 (over z, core).
Axes of the slice: x: 4, y: 8, z: 8, core: 2. Of those that a mesh axis runs over, the one named last changes fastest.
Arguments:
- movie_frames: bfloat16 [128, 1024, 4096], P('tm', 'pix'), may hold values from -48 to 48
- depth_index: int32 [1024], P('pix'), may hold values from 0 to 5
- depth_width: float32 [6], replicated, may hold values from 0.7 to 3
- temporal_test_matrix: float32 [128, 96], replicated, may hold values from -4 to 4
- merge_probe: float32 [192, 96], replicated, may hold values from -4 to 4
Outputs:
- temporal_rows: float32 [96, 128], P(None, 'tm')
- loadings: bfloat16 [96, 1024, 4096], P(None, 'pix', 'tm')
All inputs are finite; a program needn't handle non-finite values.
Results may differ from a plain program's by a relative error of at most 0.0062.
Values may be sent and summed in bfloat16 or wider, within the bound.
No kernel may reach another device: no remote copies, remote signals or barrier semaphores. Data moves between devices by JAX's collectives and lax.ppermute only.
A program may use at most 64 MiB of HBM per device.

v0:
```python
import math
import jax
import jax.numpy as jnp
from jax import lax
from jax.sharding import PartitionSpec as P

ROWS_DEV = 32
COLS = 4096
HW = 4
NDEPTH = 6
greatest_rank = lax.Precision.HIGHEST
reduction_multiplier = math.sqrt(0.5)
growth_multiplier = math.sqrt(2.0)


def with_halo(block, sides, width):
    for axis, dim in sides:
        count = lax.axis_size(axis)
        forward = [(i, i + 1) for i in range(count - 1)]
        backward = [(target, source) for source, target in forward]
        low = lax.ppermute(
            lax.slice_in_dim(block, block.shape[dim] - width, None, axis=dim), axis, forward
        )
        high = lax.ppermute(lax.slice_in_dim(block, 0, width, axis=dim), axis, backward)
        block = jnp.concatenate([low, block, high], axis=dim)
    return block


def partner_2(value, axis, distance):
    mask = 2**distance
    pairs = [(source, source ^ mask) for source in range(lax.axis_size(axis))]
    return lax.ppermute(value, axis, pairs)


def taps_table(depth_width):
    offsets = jnp.arange(-HW, HW + 1).astype(jnp.float32)
    kernel_raw = jnp.exp(-offsets[None, :] ** 2 / (2.0 * depth_width[:, None] ** 2))
    return kernel_raw / jnp.sum(kernel_raw, axis=1, keepdims=True)


def row_weights(row_depth, depth_width):
    classes = jnp.arange(NDEPTH)
    onehot = (row_depth[:, None] == classes[None, :]).astype(jnp.float32)
    return jnp.dot(onehot, taps_table(depth_width), precision=greatest_rank)


def smooth_rows(padded, weights):
    row_count = weights.shape[0]
    summed = jnp.zeros((padded.shape[0], row_count, padded.shape[2]), jnp.float32)
    for offset in range(2 * HW + 1):
        summed = summed + weights[:, offset][None, :, None] * padded[
            :, offset : offset + row_count, :
        ].astype(jnp.float32)
    return summed.astype(jnp.bfloat16)


def orthonormal(sketch):
    factor = jnp.linalg.cholesky(jnp.dot(sketch.T, sketch, precision=greatest_rank))
    return lax.linalg.triangular_solve(
        factor, sketch, left_side=False, lower=True, transpose_a=True
    )


def tile_basis(scatter_matrix, temporal_test_matrix):
    basis_cols = orthonormal(jnp.dot(scatter_matrix, temporal_test_matrix, precision=greatest_rank))
    projected = jnp.dot(basis_cols.T, scatter_matrix, precision=greatest_rank)
    inner_gram = jnp.dot(projected, basis_cols, precision=greatest_rank)
    factor = jnp.linalg.cholesky(inner_gram)
    coefficient = lax.linalg.triangular_solve(
        factor, basis_cols, left_side=False, lower=True, transpose_a=True
    )
    return (factor, projected, coefficient)


def body(movie_frames, depth_index, depth_width, temporal_test_matrix, merge_probe):
    weights = row_weights(depth_index, depth_width)
    padded = with_halo(movie_frames, (("pix", 1),), HW)
    smoothed = smooth_rows(padded, weights)
    columns = lax.all_to_all(smoothed, "tm", split_axis=2, concat_axis=0, tiled=True)
    frame_total = columns.shape[0]
    flattened = columns.reshape(frame_total, -1)
    partial_cov = lax.dot_general(
        flattened, flattened, (((1,), (1,)), ((), ())), preferred_element_type=jnp.float32
    )
    scatter_matrix = lax.psum(partial_cov, "tm") / (ROWS_DEV * COLS)
    factor, projected, coefficient = tile_basis(scatter_matrix, temporal_test_matrix)
    span_length = movie_frames.shape[0]
    span_start = lax.axis_index("tm") * span_length
    rank_count = projected.shape[0]
    tree_level_count = lax.axis_size("pix").bit_length() - 1
    pix_position = lax.axis_index("pix")
    path_product = jnp.eye(rank_count, dtype=jnp.float32)
    own_projected = lax.dynamic_slice_in_dim(projected, span_start, span_length, 1)
    own_rows = lax.linalg.triangular_solve(factor, own_projected, left_side=True, lower=True)
    for merge_level in range(tree_level_count):
        partner = partner_2(own_rows, "pix", merge_level)
        is_first = pix_position >> merge_level & 1 == 0
        first_rows = jnp.where(is_first, own_rows, partner)
        second_rows = jnp.where(is_first, partner, own_rows)
        stacked = jnp.concatenate([first_rows, second_rows], axis=0)
        stacked_gram = lax.psum(jnp.dot(stacked, stacked.T, precision=greatest_rank), "tm")
        rotation = orthonormal(jnp.dot(stacked_gram, merge_probe, precision=greatest_rank))
        own_rows = jnp.dot(rotation.T, stacked, precision=greatest_rank) * reduction_multiplier
        rotation_block = (
            jnp.where(is_first, rotation[:rank_count], rotation[rank_count:]) * growth_multiplier
        )
        path_product = jnp.dot(path_product, rotation_block, precision=greatest_rank)
    weights_table = jnp.dot(coefficient, path_product, precision=greatest_rank).astype(jnp.bfloat16)
    loading_flat = lax.dot_general(
        weights_table, flattened, (((0,), (0,)), ((), ())), preferred_element_type=jnp.float32
    )
    loadings = loading_flat.astype(jnp.bfloat16).reshape(
        rank_count, columns.shape[1], columns.shape[2]
    )
    return (own_rows, loadings)


def solution(mesh):
    in_specs = (P("tm", "pix", None), P("pix"), P(), P(), P())
    out_specs = (P(None, "tm"), P(None, "pix", "tm"))
    return jax.shard_map(body, mesh=mesh, in_specs=in_specs, out_specs=out_specs, check_vma=False)
```

profile of v0, /device:TPU:1, one launch (start us, length us, event | category | flops | bytes accessed | tf_op | source)
XLA Modules:
  0.0 986.0 jit_solution(14767062543887843147)
XLA Ops:
  7.3 1.6 fusion.105
  9.0 1.3 collective-permute-start.1
  10.5 4.7 collective-permute-start
  15.2 1.7 constant_dynamic-update-slice_fusion
  17.4 1.0 collective-permute-done
  19.0 6.4 add_convert_fusion
  25.3 9.2 copy.75
  34.5 13.4 %reshape.80 = bf16[16,2,32768]{2,1,0:T(2,128)(2,1)S(1)} reshape(bf16[4096,8,32]{2,1,0:T(8,128)(2,1)} %bitcast.158) | data formatting | bytes 4194304
  47.9 64.5 %all_to_all.15 = bf16[16,2,32768]{2,1,0:T(2,128)(2,1)} all-to-all(bf16[16,2,32768]{2,1,0:T(2,128)(2,1)S(1)} %reshape.80), channel_id=1, replica_groups=mesh['pix'=32,'tm'=16] {'tm'}, dimensions={0} | all-to-all | bytes 4194304 | tf_op jit(solution)/shard_map/all_to_all | solution.py:79
  112.4 12.9 %reshape.81 = bf16[4096,8,32]{2,1,0:T(8,128)(2,1)} reshape(bf16[16,2,32768]{2,1,0:T(2,128)(2,1)} %all_to_all.15) | data formatting | bytes 4194304
  125.3 8.8 copy.86
  134.2 1.3 fusion.106
  135.9 105.2 %all-reduce.7.cloned.1.call-done = f32[128,128]{1,0:T(8,128)} async-done(((f32[128,128]{1,0:T(8,128)}), f32[128,128]{1,0:T(8,128)}) %all-reduce.7.cloned.1.call-update) | async-done | bytes 65552 | tf_op jit(solution)/shard_map/psum | solution.py:85
  241.1 1.1 fusion.5
  242.5 8.8 cholesky.119
  251.3 0.6 compare_reduce_fusion.6
  252.0 0.7 fusion.7
  252.6 7.4 custom-call.17
  260.2 1.0 fusion.3
  261.6 8.8 cholesky.130
  271.1 0.7 fusion.8
  271.7 7.4 custom-call.11
  279.4 3.1 collective-permute-start.2
  282.5 1.2 collective-permute-done.2
  283.8 1.1 fusion.81
  285.5 110.7 %all-reduce.9.cloned.1.call-done = f32[192,192]{1,0:T(8,128)} async-done(((f32[192,192]{1,0:T(8,128)}), f32[192,192]{1,0:T(8,128)}) %all-reduce.9.cloned.1.call-update) | async-done | bytes 147472 | tf_op jit(solution)/shard_map/psum | solution.py:101
  396.1 1.2 fusion.109
  397.9 8.8 cholesky.141
  407.3 0.7 fusion.9
  408.0 7.4 custom-call.18
  415.9 4.1 collective-permute-start.3
  420.0 1.2 collective-permute-done.3
  421.2 1.1 fusion.80
  422.4 113.0 %all-reduce.11.cloned.1.call-done = f32[192,192]{1,0:T(8,128)} async-done(((f32[192,192]{1,0:T(8,128)}), f32[192,192]{1,0:T(8,128)}) %all-reduce.11.cloned.1.call-update) | async-done | bytes 147472 | tf_op jit(solution)/shard_map/psum | solution.py:101
  535.4 1.2 fusion.111
  537.1 8.8 cholesky.152
  546.6 0.7 fusion.10
  547.2 7.4 custom-call.19
  555.1 7.1 collective-permute-start.4
  562.3 1.1 collective-permute-done.4
  563.4 1.1 fusion.79
  565.1 112.5 %all-reduce.13.cloned.1.call-done = f32[192,192]{1,0:T(8,128)} async-done(((f32[192,192]{1,0:T(8,128)}), f32[192,192]{1,0:T(8,128)}) %all-reduce.13.cloned.1.call-update) | async-done | bytes 147472 | tf_op jit(solution)/shard_map/psum | solution.py:101
  677.6 1.2 fusion.113
  679.3 8.8 cholesky.163
  688.8 0.7 fusion.11
  689.5 7.4 custom-call.20
  697.4 3.1 collective-permute-start.5
  700.8 1.0 collective-permute-done.5
  701.8 1.1 fusion.78
  703.3 112.7 %all-reduce.15.cloned.1.call-done = f32[192,192]{1,0:T(8,128)} async-done(((f32[192,192]{1,0:T(8,128)}), f32[192,192]{1,0:T(8,128)}) %all-reduce.15.cloned.1.call-update) | async-done | bytes 147472 | tf_op jit(solution)/shard_map/psum | solution.py:101
  816.0 1.2 fusion.115
  817.7 8.8 cholesky.174
  827.2 0.7 fusion.12
  827.8 7.4 custom-call.21
  835.7 4.9 collective-permute-start.6
  840.9 0.7 collective-permute-done.6
  841.6 1.1 fusion.77
  843.1 112.7 %all-reduce.17.cloned.1.call-done = f32[192,192]{1,0:T(8,128)} async-done(((f32[192,192]{1,0:T(8,128)}), f32[192,192]{1,0:T(8,128)}) %all-reduce.17.cloned.1.call-update) | async-done | bytes 147472 | tf_op jit(solution)/shard_map/psum | solution.py:101
  955.8 1.2 fusion.117
  957.5 8.8 cholesky.185
  967.0 0.7 fusion.13
  967.6 7.4 custom-call.22
  975.4 0.8 convolution_multiply_fusion
  977.3 1.6 copy.87
  (90 shorter events, 15.4 us)
Async XLA Ops:
  7.2 389.0 %copy-start = (f32[192,96]{1,0:T(8,128)S(1)}, f32[192,96]{1,0:T(8,128)}, u32[]{:S(2)}) copy-start(f32[192,96]{1,0:T(8,128)} %param.14) | copy-start | bytes 221188
  7.2 11.8 %copy-start.1 = (bf16[8,32,4096]{2,1,0:T(8,128)(2,1)S(1)}, bf16[8,32,4096]{2,1,0:T(8,128)(2,1)}, u32[]{:S(2)}) copy-start(bf16[8,32,4096]{2,1,0:T(8,128)(2,1)} %param.10) | copy-start | bytes 6291460
  7.2 9.7 copy-start.3
  7.2 9.9 %copy-start.4 = (s32[32]{0:T(128)S(1)}, s32[32]{0:T(128)}, u32[]{:S(2)}) copy-start(s32[32]{0:T(128)} %param.11) | copy-start | bytes 388
  7.2 233.9 %all-reduce.7.cloned.1.call-start = ((), (), s32[]{:S(2)}) async-start(), calls=%async_computation.1 | async-start | bytes 131072 | tf_op jit(solution)/shard_map/psum | solution.py:85
  9.0 9.6 collective-permute-start.1
  10.5 8.0 collective-permute-start
  134.2 106.9 %copy-start.2 = (f32[128,96]{0,1:T(8,128)S(1)}, f32[128,96]{0,1:T(8,128)}, u32[]{:S(2)}) copy-start(f32[128,96]{0,1:T(8,128)} %param.13) | copy-start | bytes 147460
  135.5 260.6 %all-reduce.9.cloned.1.call-start = ((), (), s32[]{:S(2)}) async-start(), calls=%async_computation.2 | async-start | bytes 393216 | tf_op jit(solution)/shard_map/psum | solution.py:101
  279.4 4.4 collective-permute-start.2
  284.9 250.5 %all-reduce.11.cloned.1.call-start = ((), (), s32[]{:S(2)}) async-start(), calls=%async_computation.3 | async-start | bytes 393216 | tf_op jit(solution)/shard_map/psum | solution.py:101
  415.9 5.3 collective-permute-start.3
  422.3 255.3 %all-reduce.13.cloned.1.call-start = ((), (), s32[]{:S(2)}) async-start(), calls=%async_computation.4 | async-start | bytes 393216 | tf_op jit(solution)/shard_map/psum | solution.py:101
  555.1 8.3 collective-permute-start.4
  564.6 251.4 %all-reduce.15.cloned.1.call-start = ((), (), s32[]{:S(2)}) async-start(), calls=%async_computation.5 | async-start | bytes 393216 | tf_op jit(solution)/shard_map/psum | solution.py:101
  697.4 4.4 collective-permute-start.5
  702.9 252.9 %all-reduce.17.cloned.1.call-start = ((), (), s32[]{:S(2)}) async-start(), calls=%async_computation.6 | async-start | bytes 393216 | tf_op jit(solution)/shard_map/psum | solution.py:101
  835.7 5.9 collective-permute-start.6
Sparse Core Ops, SparseCore 0:
  135.7 105.3 all-reduce.6
  285.0 111.0 all-reduce.8
  422.5 112.8 all-reduce.10
  564.7 112.8 all-reduce.12
  703.0 112.8 all-reduce.14
  842.9 112.8 all-reduce.16
where the time goes:
time: 992 us; the launch traced here: 986 us
  waiting for transfers between devices  673 us (68%)
  other arithmetic  129 us (13%)
  blocking collectives  64.5 us (7%)
  local copies, waits for them, and re-layouts  50.7 us (5%)
  starting transfers between devices  29.5 us (3%)
  matrix products  24.3 us (2%)
  between operations  15 us (2%)
    psum x5, waiting for transfers between devices, body(): lax.psum(jnp.dot(stacked, stacked.T, precision=greatest_rank), 'tm')  562 us
    psum x1, waiting for transfers between devices, body(): scatter_matrix = lax.psum(partial_cov, 'tm') / (ROWS_DEV * COLS)  105 us
    all_to_all x1, blocking collectives, body(): lax.all_to_all(smoothed, 'tm', split_axis=2, concat_axis=0, tiled=True)  64.5 us
    another operation x18, other arithmetic, orthonormal(): jnp.linalg.cholesky(jnp.dot(sketch.T, sketch, precision=greatest_rank))  56.7 us
    another operation x12, other arithmetic, orthonormal(): lax.linalg.triangular_solve(factor, sketch, left_side=False, lower=True,...  48.1 us
    unnamed x17, local copies, waits for them, and re-layouts  38.8 us
    ppermute x5, starting transfers between devices, partner_2(): return lax.ppermute(value, axis, pairs)  22.3 us
  transfers between devices with their start and end apart: 13, of which 12 were waited for; matrix products, arithmetic and copies ran while one was open for 0% of the time, Pallas kernels for 0%

commit v1 on v0

--- a/solution.py
+++ b/solution.py
@@ -82,7 +82,7 @@
     partial_cov = lax.dot_general(
         flattened, flattened, (((1,), (1,)), ((), ())), preferred_element_type=jnp.float32
     )
-    scatter_matrix = lax.psum(partial_cov, "tm") / (ROWS_DEV * COLS)
+    scatter_matrix = jnp.sum(lax.all_gather(partial_cov, "tm"), axis=0) / (ROWS_DEV * COLS)
     factor, projected, coefficient = tile_basis(scatter_matrix, temporal_test_matrix)
     span_length = movie_frames.shape[0]
     span_start = lax.axis_index("tm") * span_length

time: 992 us -> 927 us (0.934)
  waiting for transfers between devices: 673 us -> 609 us
    psum x1 -> x0, waiting for transfers between devices: 105 us -> none  [body(): scatter_matrix = lax.psum(partial_cov, 'tm') / (ROWS_DEV * COLS)]
    all_gather x0 -> x1, waiting for transfers between devices: none -> 40.9 us  [body(): lax.all_gather(partial_cov, 'tm')]
where the time goes in v1:
time: 927 us; the launch traced here: 921 us
  waiting for transfers between devices  609 us (66%)
  other arithmetic  130 us (14%)
  blocking collectives  64.5 us (7%)
  local copies, waits for them, and re-layouts  50.7 us (5%)
  starting transfers between devices  29.5 us (3%)
  matrix products  22.6 us (2%)
  between operations  15 us (2%)
    psum x5, waiting for transfers between devices, body(): lax.psum(jnp.dot(stacked, stacked.T, precision=greatest_rank), 'tm')  561 us
    all_to_all x1, blocking collectives, body(): lax.all_to_all(smoothed, 'tm', split_axis=2, concat_axis=0, tiled=True)  64.5 us
    another operation x18, other arithmetic, orthonormal(): jnp.linalg.cholesky(jnp.dot(sketch.T, sketch, precision=greatest_rank))  56.7 us
    another operation x12, other arithmetic, orthonormal(): lax.linalg.triangular_solve(factor, sketch, left_side=False, lower=True,...  48.1 us
    all_gather x1, waiting for transfers between devices, body(): lax.all_gather(partial_cov, 'tm')  40.9 us
    unnamed x17, local copies, waits for them, and re-layouts  38.8 us
    ppermute x5, starting transfers between devices, partner_2(): return lax.ppermute(value, axis, pairs)  22.3 us
  transfers between devices with their start and end apart: 13, of which 12 were waited for; matrix products, arithmetic and copies ran while one was open for 0% of the time, Pallas kernels for 0%

profile of v1, /device:TPU:1, one launch (start us, length us, event | category | flops | bytes accessed | tf_op | source)
XLA Modules:
  0.0 921.2 jit_solution(603261771021720269)
XLA Ops:
  7.3 1.6 fusion.105
  9.0 1.3 collective-permute-start.1
  10.5 4.7 collective-permute-start
  15.2 1.7 constant_dynamic-update-slice_fusion
  17.4 1.0 collective-permute-done
  19.0 6.4 add_convert_fusion
  25.3 9.2 copy.75
  34.5 13.4 %reshape.81 = bf16[16,2,32768]{2,1,0:T(2,128)(2,1)S(1)} reshape(bf16[4096,8,32]{2,1,0:T(8,128)(2,1)} %bitcast.159) | data formatting | bytes 4194304
  47.9 64.5 %all_to_all.15 = bf16[16,2,32768]{2,1,0:T(2,128)(2,1)} all-to-all(bf16[16,2,32768]{2,1,0:T(2,128)(2,1)S(1)} %reshape.81), channel_id=1, replica_groups=mesh['pix'=32,'tm'=16] {'tm'}, dimensions={0} | all-to-all | bytes 4194304 | tf_op jit(solution)/shard_map/all_to_all | solution.py:79
  112.4 12.9 %reshape.82 = bf16[4096,8,32]{2,1,0:T(8,128)(2,1)} reshape(bf16[16,2,32768]{2,1,0:T(2,128)(2,1)} %all_to_all.15) | data formatting | bytes 4194304
  125.3 8.8 copy.86
  134.2 1.3 fusion.106
  135.9 40.9 %all-gather.3.cloned.1.call-done = f32[2048,128]{1,0:T(8,128)} async-done(((f32[128,128]{1,0:T(8,128)}), f32[2048,128]{1,0:T(8,128)}) %all-gather.3.cloned.1.call-update) | async-done | bytes 1048592 | tf_op jit(solution)/shard_map/all_gather | solution.py:85
  176.7 1.3 reduce_sum.19
  178.6 8.8 cholesky.119
  187.4 0.6 compare_reduce_fusion.6
  188.1 0.7 fusion.7
  188.7 7.4 custom-call.17
  196.9 8.8 cholesky.130
  205.7 0.6 compare_reduce_fusion.5
  206.4 0.7 fusion.8
  207.0 7.4 custom-call.11
  214.7 3.1 collective-permute-start.2
  217.8 1.2 collective-permute-done.2
  219.1 1.1 fusion.81
  220.8 110.6 %all-reduce.6.cloned.1.call-done = f32[192,192]{1,0:T(8,128)} async-done(((f32[192,192]{1,0:T(8,128)}), f32[192,192]{1,0:T(8,128)}) %all-reduce.6.cloned.1.call-update) | async-done | bytes 147472 | tf_op jit(solution)/shard_map/psum | solution.py:101
  331.4 1.2 fusion.109
  333.1 8.8 cholesky.141
  342.5 0.7 fusion.9
  343.2 7.4 custom-call.18
  351.1 4.1 collective-permute-start.3
  355.2 1.2 collective-permute-done.3
  356.4 1.1 fusion.80
  357.6 113.0 %all-reduce.8.cloned.1.call-done = f32[192,192]{1,0:T(8,128)} async-done(((f32[192,192]{1,0:T(8,128)}), f32[192,192]{1,0:T(8,128)}) %all-reduce.8.cloned.1.call-update) | async-done | bytes 147472 | tf_op jit(solution)/shard_map/psum | solution.py:101
  470.6 1.2 fusion.111
  472.3 8.8 cholesky.152
  481.8 0.7 fusion.10
  482.4 7.4 custom-call.19
  490.4 7.1 collective-permute-start.4
  497.5 1.1 collective-permute-done.4
  498.7 1.1 fusion.79
  500.3 112.5 %all-reduce.10.cloned.1.call-done = f32[192,192]{1,0:T(8,128)} async-done(((f32[192,192]{1,0:T(8,128)}), f32[192,192]{1,0:T(8,128)}) %all-reduce.10.cloned.1.call-update) | async-done | bytes 147472 | tf_op jit(solution)/shard_map/psum | solution.py:101
  612.8 1.2 fusion.113
  614.6 8.8 cholesky.163
  624.0 0.7 fusion.11
  624.7 7.4 custom-call.20
  632.6 3.1 collective-permute-start.5
  636.0 1.0 collective-permute-done.5
  637.0 1.1 fusion.78
  638.5 112.7 %all-reduce.12.cloned.1.call-done = f32[192,192]{1,0:T(8,128)} async-done(((f32[192,192]{1,0:T(8,128)}), f32[192,192]{1,0:T(8,128)}) %all-reduce.12.cloned.1.call-update) | async-done | bytes 147472 | tf_op jit(solution)/shard_map/psum | solution.py:101
  751.1 1.2 fusion.115
  752.9 8.8 cholesky.174
  762.3 0.7 fusion.12
  763.0 7.4 custom-call.21
  770.9 4.9 collective-permute-start.6
  776.1 0.7 collective-permute-done.6
  776.8 1.1 fusion.77
  778.3 112.7 %all-reduce.14.cloned.1.call-done = f32[192,192]{1,0:T(8,128)} async-done(((f32[192,192]{1,0:T(8,128)}), f32[192,192]{1,0:T(8,128)}) %all-reduce.14.cloned.1.call-update) | async-done | bytes 147472 | tf_op jit(solution)/shard_map/psum | solution.py:101
  891.0 1.2 fusion.117
  892.7 8.8 cholesky.185
  902.2 0.7 fusion.13
  902.8 7.4 custom-call.22
  910.6 0.8 convolution_multiply_fusion
  912.5 1.6 copy.87
  (91 shorter events, 15.2 us)
Async XLA Ops:
  7.2 324.2 %copy-start = (f32[192,96]{1,0:T(8,128)S(1)}, f32[192,96]{1,0:T(8,128)}, u32[]{:S(2)}) copy-start(f32[192,96]{1,0:T(8,128)} %param.14) | copy-start | bytes 221188
  7.2 11.8 %copy-start.1 = (bf16[8,32,4096]{2,1,0:T(8,128)(2,1)S(1)}, bf16[8,32,4096]{2,1,0:T(8,128)(2,1)}, u32[]{:S(2)}) copy-start(bf16[8,32,4096]{2,1,0:T(8,128)(2,1)} %param.10) | copy-start | bytes 6291460
  7.2 9.7 %copy-start.3 = (f32[6]{0:T(128)S(1)}, f32[6]{0:T(128)}, u32[]{:S(2)}) copy-start(f32[6]{0:T(128)} %param.12) | copy-start | bytes 76
  7.2 9.9 %copy-start.4 = (s32[32]{0:T(128)S(1)}, s32[32]{0:T(128)}, u32[]{:S(2)}) copy-start(s32[32]{0:T(128)} %param.11) | copy-start | bytes 388
  7.2 169.5 %all-gather.3.cloned.1.call-start = ((), (), s32[]{:S(2)}) async-start(), calls=%async_computation.6 | async-start | bytes 1114112 | tf_op jit(solution)/shard_map/all_gather | solution.py:85
  9.0 9.6 %collective-permute-start.1 = (bf16[8,4,4096]{2,0,1:T(8,128)(2,1)S(1)}, bf16[8,4,4096]{2,0,1:T(8,128)(2,1)S(1)}, u32[]{:S(2)}, u32[]{:S(2)}) collective-permute-start(bf16[8,4,4096]{2,0,1:T(8,128)(2,1)S(1)} %copy.85), channel_id=1, source_target_pairs={{16,0},{32,16},{48,32},{64,48},{80,64},{96,80},{112,96},{128,112},... | collective-permute-start | bytes 786440 | tf_op jit(solution)/shard_map/ppermute | solution.py:24
  10.5 8.0 collective-permute-start
  134.2 43.9 %copy-start.2 = (f32[128,96]{0,1:T(8,128)S(1)}, f32[128,96]{0,1:T(8,128)}, u32[]{:S(2)}) copy-start(f32[128,96]{0,1:T(8,128)} %param.13) | copy-start | bytes 147460
  135.5 195.8 %all-reduce.6.cloned.1.call-start = ((), (), s32[]{:S(2)}) async-start(), calls=%async_computation.1 | async-start | bytes 393216 | tf_op jit(solution)/shard_map/psum | solution.py:101
  214.7 4.4 collective-permute-start.2
  220.2 250.4 %all-reduce.8.cloned.1.call-start = ((), (), s32[]{:S(2)}) async-start(), calls=%async_computation.2 | async-start | bytes 393216 | tf_op jit(solution)/shard_map/psum | solution.py:101
  351.1 5.3 collective-permute-start.3
  357.6 255.3 %all-reduce.10.cloned.1.call-start = ((), (), s32[]{:S(2)}) async-start(), calls=%async_computation.3 | async-start | bytes 393216 | tf_op jit(solution)/shard_map/psum | solution.py:101
  490.4 8.3 collective-permute-start.4
  499.8 251.3 %all-reduce.12.cloned.1.call-start = ((), (), s32[]{:S(2)}) async-start(), calls=%async_computation.4 | async-start | bytes 393216 | tf_op jit(solution)/shard_map/psum | solution.py:101
  632.6 4.4 collective-permute-start.5
  638.1 252.8 %all-reduce.14.cloned.1.call-start = ((), (), s32[]{:S(2)}) async-start(), calls=%async_computation.5 | async-start | bytes 393216 | tf_op jit(solution)/shard_map/psum | solution.py:101
  770.9 5.9 collective-permute-start.6
Sparse Core Ops, SparseCore 0:
  135.7 41.0 all-gather.2
  220.3 110.9 all-reduce.5
  357.7 112.8 all-reduce.7
  499.9 112.8 all-reduce.9
  638.2 112.8 all-reduce.11
  778.1 112.8 all-reduce.13
